TPU v7x, 32 devices: a whole 2x2x4 slice. The times are simulated.
32 devices in a mesh: dp: 8 (over y, x, core), tensor: 4 (over z).
Axes of the slice: x: 2, y: 2, z: 4, core: 2. Of those that a mesh axis runs over, the one named last changes fastest.
Arguments:
- inputs: bfloat16 [8, 1024, 768], P('dp', 'tensor'), may hold values from -6 to 6
- ln_gain: float32 [768], P(('dp', 'tensor')), may hold values from 0.25 to 1.75
- ln_bias: float32 [768], P(('dp', 'tensor')), may hold values from -1.5 to 1.5
- w_qkv: bfloat16 [768, 3, 768], P('dp', None, 'tensor'), may hold values from -1.5 to 1.5, as said below
- b_qkv: bfloat16 [3, 12, 64], P(None, 'tensor', 'dp'), may hold values from -2.5 to 2.5
- w_out: bfloat16 [768, 768], P('tensor', 'dp'), may hold values from -0.875 to 0.875
- w_in: bfloat16 [768, 3072], P('dp', 'tensor'), may hold values from -0.21875 to 0.21875
- b_in: bfloat16 [24, 128], P('tensor', 'dp'), may hold values from -2.5 to 2.5
- w_down: bfloat16 [3072, 768], P('tensor', 'dp'), may hold values from -0.109375 to 0.109375
- out_bias: float32 [2, 768], P(None, ('dp', 'tensor')), may hold values from -2.5 to 2.5
- cotangent: bfloat16 [8, 1024, 768], P('dp', 'tensor'), may hold values from -6 to 6
Outputs:
- outputs: bfloat16 [8, 1024, 768], P('dp', 'tensor')
- input_grad: bfloat16 [8, 1024, 768], P('dp', 'tensor')
- ln_gain_grad: float32 [768], P(('dp', 'tensor'))
- ln_bias_grad: float32 [768], P(('dp', 'tensor'))
- w_qkv_grad: float32 [768, 3, 768], P('dp', None, 'tensor')
- b_qkv_grad: float32 [3, 12, 64], P(None, 'tensor', 'dp')
- w_out_grad: float32 [768, 768], P('tensor', 'dp')
- w_in_grad: float32 [768, 3072], P('dp', 'tensor')
- b_in_grad: float32 [24, 128], P('tensor', 'dp')
- w_down_grad: float32 [3072, 768], P('tensor', 'dp')
- out_bias_grad: float32 [2, 768], P(None, ('dp', 'tensor'))
Inputs may be any that keep to these rules, and one draw needn't show every extreme that they name: `w_qkv`: projection weights of the queries, keys and values.
All inputs are finite; a program needn't handle non-finite values.
Results may differ from a plain program's by a relative error of at most 0.0082.
Values may be sent and summed in bfloat16 or wider, within the bound.
No kernel may reach another device: no remote copies, remote signals or barrier semaphores. Data moves between devices by JAX's collectives and lax.ppermute only.
A program may use at most 128 MiB of HBM per device.

v0:
```python
import math
import jax
import jax.numpy as jnp
from jax import lax
from jax.sharding import PartitionSpec as P

ROT = 16
EPS = 1e-05
ROOT_HALF = 0.7071067811865476
INV_ROOT_TAU = 0.3989422804014327
NEG_BIG = -1e30


def rotary_tables(length, rot_dims):
    half_rot = rot_dims // 2
    position = jnp.arange(length).astype(jnp.float32)
    inv_freq = jnp.exp(
        jnp.arange(half_rot).astype(jnp.float32) * (-2.0 * math.log(10000.0) / rot_dims)
    )
    angles = position[:, None] * inv_freq[None, :]
    return (jnp.cos(angles), jnp.sin(angles))


def rotate(tensor_in, cosine_table, sine_table, rot_dims, direction):
    half_rot = rot_dims // 2
    first_half = tensor_in[..., :half_rot]
    second_half = tensor_in[..., half_rot:rot_dims]
    cos_rows = cosine_table[:, None, :]
    sin_rows = sine_table[:, None, :] * direction
    return jnp.concatenate(
        [
            first_half * cos_rows - second_half * sin_rows,
            second_half * cos_rows + first_half * sin_rows,
            tensor_in[..., rot_dims:],
        ],
        axis=-1,
    )


def gelu_parts(pre_act):
    normal_cdf = 0.5 * (1.0 + lax.erf(pre_act * ROOT_HALF))
    normal_pdf = jnp.exp(-0.5 * pre_act * pre_act) * INV_ROOT_TAU
    return (pre_act * normal_cdf, normal_cdf + pre_act * normal_pdf)


def masked_scores(q_rows, key_rows, first_row, block_rows, length):
    head_dim = q_rows.shape[-1]
    scores = jnp.einsum(
        "qhd,khd->hqk", q_rows, key_rows, preferred_element_type=jnp.float32
    ) / math.sqrt(head_dim)
    key_pos = jnp.arange(length)
    allowed = (first_row + jnp.arange(block_rows))[:, None] >= key_pos[None, :]
    return jnp.where(allowed[None], scores, NEG_BIG)


def attend(triple):
    queries, key_rows, value_rows = triple
    length = queries.shape[0]
    block_rows = min(512, length)

    def one_block(first_row):
        q_rows = lax.dynamic_slice_in_dim(queries, first_row, block_rows, 0)
        scores = masked_scores(q_rows, key_rows, first_row, block_rows, length)
        row_max = jnp.max(scores, axis=-1, keepdims=True)
        exponent = jnp.exp(scores - row_max)
        row_total = jnp.sum(exponent, axis=-1, keepdims=True)
        attn_probs = (exponent / row_total).astype(jnp.bfloat16)
        context = jnp.einsum(
            "hqk,khd->qhd", attn_probs, value_rows, preferred_element_type=jnp.float32
        )
        return (context.astype(jnp.bfloat16), (row_max + jnp.log(row_total))[..., 0])

    starts = jnp.arange(length // block_rows) * block_rows
    context, logsum = lax.map(one_block, starts)
    return (context.reshape(queries.shape), logsum)


def attend_back(group):
    queries, key_rows, value_rows, logsum, ctx_grad = group
    length = queries.shape[0]
    block_rows = min(512, length)
    head_dim = queries.shape[-1]

    def one_block(carry, block_index):
        key_grad, value_grad = carry
        first_row = block_index * block_rows
        q_rows = lax.dynamic_slice_in_dim(queries, first_row, block_rows, 0)
        d_rows = lax.dynamic_slice_in_dim(ctx_grad, first_row, block_rows, 0)
        scores = masked_scores(q_rows, key_rows, first_row, block_rows, length)
        attn_probs = jnp.exp(scores - logsum[block_index][..., None])
        value_grad = value_grad + jnp.einsum(
            "hqk,qhd->khd",
            attn_probs.astype(jnp.bfloat16),
            d_rows,
            preferred_element_type=jnp.float32,
        )
        prob_grad = jnp.einsum(
            "qhd,khd->hqk", d_rows, value_rows, preferred_element_type=jnp.float32
        )
        row_dot = jnp.sum(attn_probs * prob_grad, axis=-1, keepdims=True)
        score_grad = (attn_probs * (prob_grad - row_dot) / math.sqrt(head_dim)).astype(jnp.bfloat16)
        query_grad = jnp.einsum(
            "hqk,khd->qhd", score_grad, key_rows, preferred_element_type=jnp.float32
        )
        key_grad = key_grad + jnp.einsum(
            "hqk,qhd->khd", score_grad, q_rows, preferred_element_type=jnp.float32
        )
        return ((key_grad, value_grad), query_grad)

    zero_grads = jnp.zeros(queries.shape, jnp.float32)
    (key_grad, value_grad), query_grad = lax.scan(
        one_block, (zero_grads, zero_grads), jnp.arange(length // block_rows)
    )
    return (query_grad.reshape(queries.shape), key_grad, value_grad)


def body(inputs, ln_gain, ln_bias, w_qkv, b_qkv, w_out, w_in, b_in, w_down, out_bias, cotangent):
    gain, shift, biases = (
        lax.all_gather(ln_gain, ("dp", "tensor"), axis=0, tiled=True),
        lax.all_gather(ln_bias, ("dp", "tensor"), axis=0, tiled=True),
        lax.all_gather(out_bias, ("dp", "tensor"), axis=1, tiled=True),
    )
    forward_weights = (
        lax.all_gather(w_qkv, "dp", axis=0, tiled=True),
        lax.all_gather(b_qkv, "dp", axis=2, tiled=True),
        lax.all_gather(w_out, "dp", axis=1, tiled=True),
        lax.all_gather(w_in, "dp", axis=0, tiled=True),
        lax.all_gather(b_in, "dp", axis=1, tiled=True),
        lax.all_gather(w_down, "dp", axis=1, tiled=True),
    )
    qkv_full, qkv_bias, out_full, in_full, in_bias, down_full = forward_weights
    model = qkv_full.shape[0]
    heads = qkv_bias.shape[1]
    head_dim = qkv_bias.shape[2]
    local_width = heads * head_dim
    hidden_units = in_full.shape[1]
    input_full = inputs.astype(jnp.float32)
    centred = input_full - jnp.mean(input_full, axis=-1, keepdims=True)
    inv_sigma = lax.rsqrt(jnp.mean(centred * centred, axis=-1, keepdims=True) + EPS)
    unit_rows = centred * inv_sigma
    normed = (unit_rows * gain + shift).astype(jnp.bfloat16)
    gathered = lax.all_gather(normed, "tensor", axis=1, tiled=True)
    seqs = gathered.shape[0]
    length = gathered.shape[1]
    total_rows = seqs * length
    flat_normed = gathered.reshape(total_rows, model)
    qkv_matrix = qkv_full.reshape(model, 3 * local_width)
    projected = jnp.dot(flat_normed, qkv_matrix, preferred_element_type=jnp.float32)
    projected = projected.reshape(seqs, length, 3, heads, head_dim) + qkv_bias.astype(jnp.float32)
    cosine_table, sine_table = rotary_tables(length, ROT)
    queries = rotate(projected[:, :, 0], cosine_table, sine_table, ROT, 1.0).astype(jnp.bfloat16)
    key_rows = rotate(projected[:, :, 1], cosine_table, sine_table, ROT, 1.0).astype(jnp.bfloat16)
    value_rows = projected[:, :, 2].astype(jnp.bfloat16)
    context, logsum = lax.map(attend, (queries, key_rows, value_rows))
    flat_ctx = context.reshape(total_rows, local_width)
    pre_act = jnp.dot(flat_normed, in_full, preferred_element_type=jnp.float32) + in_bias.astype(
        jnp.float32
    ).reshape(hidden_units)
    activated, slopes = gelu_parts(pre_act)
    hidden = activated.astype(jnp.bfloat16)
    branch = jnp.dot(flat_ctx, out_full, preferred_element_type=jnp.float32) + jnp.dot(
        hidden, down_full, preferred_element_type=jnp.float32
    )
    summed = lax.psum_scatter(
        branch.reshape(seqs, length, model), "tensor", scatter_dimension=1, tiled=True
    )
    outputs = (input_full + summed + biases[0] + biases[1]).astype(jnp.bfloat16)
    cot_rows = lax.all_gather(cotangent, "tensor", axis=1, tiled=True)
    flat_cot = cot_rows.reshape(total_rows, model)
    backward_weights = (
        lax.all_gather(w_qkv, "dp", axis=0, tiled=True),
        lax.all_gather(b_qkv, "dp", axis=2, tiled=True),
        lax.all_gather(w_out, "dp", axis=1, tiled=True),
        lax.all_gather(w_in, "dp", axis=0, tiled=True),
        lax.all_gather(b_in, "dp", axis=1, tiled=True),
        lax.all_gather(w_down, "dp", axis=1, tiled=True),
    )
    qkv_back, bias_back, out_back, in_back, in_bias_back, down_back = backward_weights
    left_dims = (((0,), (0,)), ((), ()))
    right_dims = (((1,), (1,)), ((), ()))
    grad_down = lax.dot_general(hidden, flat_cot, left_dims, preferred_element_type=jnp.float32)
    pre_grad = (
        lax.dot_general(flat_cot, down_back, right_dims, preferred_element_type=jnp.float32)
        * slopes
    )
    pre_low = pre_grad.astype(jnp.bfloat16)
    grad_in = lax.dot_general(flat_normed, pre_low, left_dims, preferred_element_type=jnp.float32)
    grad_in_bias = jnp.sum(pre_grad, axis=0).reshape(in_bias_back.shape)
    grad_out = lax.dot_general(flat_ctx, flat_cot, left_dims, preferred_element_type=jnp.float32)
    ctx_grad = lax.dot_general(flat_cot, out_back, right_dims, preferred_element_type=jnp.float32)
    ctx_grad = ctx_grad.astype(jnp.bfloat16).reshape(seqs, length, heads, head_dim)
    query_grad, key_grad, value_grad = lax.map(
        attend_back, (queries, key_rows, value_rows, logsum, ctx_grad)
    )
    proj_grad = jnp.stack(
        [
            rotate(query_grad, cosine_table, sine_table, ROT, -1.0),
            rotate(key_grad, cosine_table, sine_table, ROT, -1.0),
            value_grad,
        ],
        axis=2,
    )
    grad_qkv_bias = jnp.sum(proj_grad, axis=(0, 1))
    proj_low = proj_grad.astype(jnp.bfloat16).reshape(total_rows, 3 * local_width)
    grad_qkv = lax.dot_general(flat_normed, proj_low, left_dims, preferred_element_type=jnp.float32)
    grad_qkv = grad_qkv.reshape(model, 3, local_width)
    qkv_back_matrix = qkv_back.reshape(model, 3 * local_width)
    norm_grad = lax.dot_general(
        proj_low, qkv_back_matrix, right_dims, preferred_element_type=jnp.float32
    )
    norm_grad = norm_grad + lax.dot_general(
        pre_low, in_back, right_dims, preferred_element_type=jnp.float32
    )
    own_grad = lax.psum_scatter(
        norm_grad.reshape(seqs, length, model), "tensor", scatter_dimension=1, tiled=True
    )
    unit_grad = own_grad * gain
    cot_full = cotangent.astype(jnp.float32)
    input_grad = cot_full + inv_sigma * (
        unit_grad
        - jnp.mean(unit_grad, axis=-1, keepdims=True)
        - unit_rows * jnp.mean(unit_grad * unit_rows, axis=-1, keepdims=True)
    )
    input_grad = input_grad.astype(jnp.bfloat16)
    gain_part = jnp.sum(own_grad * unit_rows, axis=(0, 1))
    shift_part = jnp.sum(own_grad, axis=(0, 1))
    bias_part = jnp.sum(cot_full, axis=(0, 1))
    bias_pair = jnp.stack([bias_part, bias_part])
    gain_grad, shift_grad, bias_grad = (
        lax.psum_scatter(gain_part, ("dp", "tensor"), scatter_dimension=0, tiled=True),
        lax.psum_scatter(shift_part, ("dp", "tensor"), scatter_dimension=0, tiled=True),
        lax.psum_scatter(bias_pair, ("dp", "tensor"), scatter_dimension=1, tiled=True),
    )
    qkv_grad_out, qkv_bias_grad_out, out_grad_out, in_grad_out, in_bias_grad_out, down_grad_out = (
        lax.psum_scatter(grad_qkv, "dp", scatter_dimension=0, tiled=True),
        lax.psum_scatter(grad_qkv_bias, "dp", scatter_dimension=2, tiled=True),
        lax.psum_scatter(grad_out, "dp", scatter_dimension=1, tiled=True),
        lax.psum_scatter(grad_in, "dp", scatter_dimension=0, tiled=True),
        lax.psum_scatter(grad_in_bias, "dp", scatter_dimension=1, tiled=True),
        lax.psum_scatter(grad_down, "dp", scatter_dimension=1, tiled=True),
    )
    return (
        outputs,
        input_grad,
        gain_grad,
        shift_grad,
        qkv_grad_out,
        qkv_bias_grad_out,
        out_grad_out,
        in_grad_out,
        in_bias_grad_out,
        down_grad_out,
        bias_grad,
    )


def solution(mesh):
    placed = (
        P("dp", "tensor", None),
        P(("dp", "tensor")),
        P(("dp", "tensor")),
        P("dp", None, "tensor"),
        P(None, "tensor", "dp"),
        P("tensor", "dp"),
        P("dp", "tensor"),
        P("tensor", "dp"),
        P("tensor", "dp"),
        P(None, ("dp", "tensor")),
        P("dp", "tensor", None),
    )
    return jax.shard_map(
        body,
        mesh=mesh,
        in_specs=placed,
        out_specs=(
            P("dp", "tensor", None),
            P("dp", "tensor", None),
            P(("dp", "tensor")),
            P(("dp", "tensor")),
            P("dp", None, "tensor"),
            P(None, "tensor", "dp"),
            P("tensor", "dp"),
            P("dp", "tensor"),
            P("tensor", "dp"),
            P("tensor", "dp"),
            P(None, ("dp", "tensor")),
        ),
        check_vma=False,
    )
```

profile of v0, /device:TPU:0, one launch (start us, length us, event | category | flops | bytes accessed | tf_op | source)
XLA Modules:
  0.0 593.6 jit_solution(9107140524121547792)
XLA Ops:
  7.2 1.1 convert_reduce_fusion
  8.4 1.2 fusion.117
  11.3 42.0 %all-reduce.7 = (f32[768]{0:T(1024)S(1)}, f32[768]{0:T(1024)S(1)}) all-reduce(f32[768]{0:T(1024)S(1)} %dynamic-update-slice.1, f32[768]{0:T(1024)S(1)} %dynamic-update-slice), channel_id=1, replica_groups=mesh['dp'=8,'tensor'=4] {'dp','tensor'}, use_global_device_ids=true, to_apply=%add.1 | all-reduce | flops 1536 | bytes 12288
  53.4 2.0 fusion.112
  57.7 1.0 copy.40
  58.7 12.8 %all_gather.40 = bf16[768,3,192]{2,1,0:T(4,128)(2,1)S(1)} all-gather(bf16[96,3,192]{2,1,0:T(4,128)(2,1)S(1)} %copy.40), channel_id=1, replica_groups=mesh['dp'=8,'tensor'=4] {'dp'}, dimensions={0}, use_global_device_ids=true | all-gather | bytes 995328 | tf_op jit(solution)/shard_map/all_gather | solution.py:124
  72.6 9.4 %all_gather.41 = bf16[3,3,64]{1,0,2:T(4,128)(2,1)S(1)} all-gather(bf16[3,3,8]{1,0,2:T(4,128)(2,1)S(1)} %copy.42), channel_id=1, replica_groups=mesh['dp'=8,'tensor'=4] {'dp'}, dimensions={2}, use_global_device_ids=true | all-gather | bytes 1296 | tf_op jit(solution)/shard_map/all_gather | solution.py:125
  82.2 8.4 %all_gather.42 = bf16[192,768]{0,1:T(8,128)(2,1)S(1)} all-gather(bf16[192,96]{0,1:T(8,128)(2,1)S(1)} %copy.45), channel_id=1, replica_groups=mesh['dp'=8,'tensor'=4] {'dp'}, dimensions={1}, use_global_device_ids=true | all-gather | bytes 331776 | tf_op jit(solution)/shard_map/all_gather | solution.py:126
  90.6 9.0 %all-gather = bf16[8,16,6]{1,2,0:T(8,128)(2,1)S(1)} all-gather(bf16[1,16,6]{1,2,0:T(8,128)(2,1)S(1)} %bitcast.195), channel_id=1, replica_groups=mesh['dp'=8,'tensor'=4] {'dp'}, dimensions={0}, use_global_device_ids=true | all-gather | bytes 1728 | tf_op jit(solution)/shard_map/all_gather | solution.py:128
  100.5 2.7 add_bitcast_fusion.2
  103.7 18.3 %while.47 = (s32[]{:T(128)}, bf16[2,512,3,64]{1,3,2,0:T(8,128)(2,1)S(1)}, f32[2,3,512]{2,1,0:T(4,128)S(1)}, s32[2]{0:T(128)S(1)}, bf16[1024,3,64]{0,2,1:T(8,128)...) while((s32[]{:T(128)}, ...), condition=%wide.region_5.6_spmd, body=%wide.region_2.5_spmd.sunk | while | flops 422149120 | bytes 22214820 | solution.py:74
  107.3 1.5 fusion.177
  108.8 1.8 fusion.178
  110.6 2.2 fusion.179
  116.4 1.5 fusion.177
  118.0 1.8 fusion.178
  119.8 2.2 fusion.179
  122.0 7.9 %all-gather.13.cloned.1.call-done = bf16[1,1024,768]{2,1,0:T(8,128)(2,1)} async-done(((bf16[1,256,768]{2,1,0:T(8,128)(2,1)}), bf16[1,1024,768]{2,1,0:T(8,128)(2,1)}) %all-gather.13.cloned.1.call-update) | async-done | bytes 1572880 | tf_op jit(solution)/shard_map/all_gather | solution.py:168
  129.9 2.1 fusion.102
  132.0 105.2 %while.48 = (s32[]{:T(128)}, f32[1024,3,64]{0,2,1:T(8,128)}, f32[1024,3,64]{0,2,1:T(8,128)}, f32[2,512,3,64]{1,0,3,2:T(2,128)}, s32[2]{0:T(128)S(1)}, /*index=5*...) while((s32[]{:T(128)}, f32[1024,3,64]{0,2,1:T(8,128)}, ...), condition=%wide.region_9.10_spmd.clone, body=%wide.region_7.9_spmd.clone.sunk | while | flops 1048843776 | bytes 72661312 | solution.py:111
  133.7 3.7 fusion.191
  137.4 3.7 fusion.190
  143.4 12.7 %fusion.194 = f32[1,512,3,64]{1,3,2,0:T(8,128)S(1)} fusion(bf16[1024,3,64]{0,2,1:T(8,128)(2,1)S(1)} %get-tuple-element.435, f32[3,512,1024]{2,1,0:T(8,128)} %fusion.190, f32[3,512,1024]{2,1,0:T(8,128)} %fusion.191, f32[3,512]{1,0:T(4,128)S(1)} %dynamic-slice_bitcast_fusion.2, pred[512,1024]{1,0:T(8,128)(4,1)S(1)} %iota_compare_fusion.5), kind=kOutput, calls=%fused_computation.40.clone.1 | convolution fusion | flops 218630656 | bytes 13899776 | tf_op jit(solution)/shard_map/while/body/eval_jaxpr/while/body/eval_jaxpr/hqk,khd->qhd/dot_general | solution.py:102
  156.5 8.1 %dynamic_update_slice.33 = f32[2,512,3,64]{1,0,3,2:T(2,128)} dynamic-update-slice(f32[2,512,3,64]{1,0,3,2:T(2,128)} %get-tuple-element.417, f32[1,512,3,64]{1,0,3,2:T(1,128)S(1)} %copy.75, s32[]{:T(128)} %get-tuple-element.414, s32[]{:T(128)} %constant.78.clone.1..sunk.1, s32[]{:T(128)} %constant.78.clone.1..sunk.1, s32[]{:T(128)} %constant.78.clone.1..sunk.1) | dynamic-update-slice | bytes 786436 | tf_op jit(solution)/shard_map/while/body/eval_jaxpr/while/body/jit(dynamic_update_index_in_dim)/dynamic_update_slice | solution.py:111
  164.6 14.4 %fusion.192 = f32[1024,3,64]{0,2,1:T(8,128)} fusion(f32[3,512,1024]{2,1,0:T(8,128)} %fusion.190, f32[3,512,1024]{2,1,0:T(8,128)} %fusion.191, f32[3,512]{1,0:T(4,128)S(1)} %dynamic-slice_bitcast_fusion.2, pred[512,1024]{1,0:T(8,128)(4,1)S(1)} %iota_compare_fusion.5, f32[1024,3,64]{0,2,1:T(8,128)} %get-tuple-element.415, pred[]{:T(512)S(6)} %compare.3, ...), kind=kOutput, calls=%fused_computation.38.clone.1 | convolution fusion | flops 219023872 | bytes 28000260 | tf_op jit(solution)/shard_map/while/body/eval_jaxpr/while/body/eval_jaxpr/hqk,qhd->khd/dot_general | solution.py:105
  179.1 4.7 fusion.193
  183.8 0.9 copy-done.5
  185.9 3.7 fusion.191
  189.6 3.7 fusion.190
  195.6 12.7 %fusion.194 = f32[1,512,3,64]{1,3,2,0:T(8,128)S(1)} fusion(bf16[1024,3,64]{0,2,1:T(8,128)(2,1)S(1)} %get-tuple-element.435, f32[3,512,1024]{2,1,0:T(8,128)} %fusion.190, f32[3,512,1024]{2,1,0:T(8,128)} %fusion.191, f32[3,512]{1,0:T(4,128)S(1)} %dynamic-slice_bitcast_fusion.2, pred[512,1024]{1,0:T(8,128)(4,1)S(1)} %iota_compare_fusion.5), kind=kOutput, calls=%fused_computation.40.clone.1 | convolution fusion | flops 218630656 | bytes 13899776 | tf_op jit(solution)/shard_map/while/body/eval_jaxpr/while/body/eval_jaxpr/hqk,khd->qhd/dot_general | solution.py:102
  208.7 8.1 %dynamic_update_slice.33 = f32[2,512,3,64]{1,0,3,2:T(2,128)} dynamic-update-slice(f32[2,512,3,64]{1,0,3,2:T(2,128)} %get-tuple-element.417, f32[1,512,3,64]{1,0,3,2:T(1,128)S(1)} %copy.75, s32[]{:T(128)} %get-tuple-element.414, s32[]{:T(128)} %constant.78.clone.1..sunk.1, s32[]{:T(128)} %constant.78.clone.1..sunk.1, s32[]{:T(128)} %constant.78.clone.1..sunk.1) | dynamic-update-slice | bytes 786436 | tf_op jit(solution)/shard_map/while/body/eval_jaxpr/while/body/jit(dynamic_update_index_in_dim)/dynamic_update_slice | solution.py:111
  216.8 14.6 %fusion.192 = f32[1024,3,64]{0,2,1:T(8,128)} fusion(f32[3,512,1024]{2,1,0:T(8,128)} %fusion.190, f32[3,512,1024]{2,1,0:T(8,128)} %fusion.191, f32[3,512]{1,0:T(4,128)S(1)} %dynamic-slice_bitcast_fusion.2, pred[512,1024]{1,0:T(8,128)(4,1)S(1)} %iota_compare_fusion.5, f32[1024,3,64]{0,2,1:T(8,128)} %get-tuple-element.415, pred[]{:T(512)S(6)} %compare.3, ...), kind=kOutput, calls=%fused_computation.38.clone.1 | convolution fusion | flops 219023872 | bytes 28000260 | tf_op jit(solution)/shard_map/while/body/eval_jaxpr/while/body/eval_jaxpr/hqk,qhd->khd/dot_general | solution.py:105
  231.4 4.7 fusion.193
  236.1 0.9 copy-done.5
  237.2 1.8 broadcast_in_dim.74
  239.0 1.4 copy.44
  240.5 5.5 multiply_convert_fusion.1
  246.0 4.9 fusion.132
  251.8 1.6 fusion.99
  253.4 1.7 multiply_subtract_fusion.1
  255.9 1.9 slice.87
  258.0 1.3 maximum_bitcast_fusion
  259.2 1.2 maximum_bitcast_fusion.1
  260.4 1.4 fusion.84
  261.8 1.4 fusion.123
  263.4 3.2 add_bitcast_fusion
  266.7 3.2 fusion.133
  269.9 2.4 add_bitcast_fusion.1
  272.3 4.6 fusion.85
  277.2 4.8 fusion.97
  282.1 4.3 fusion.88
  286.5 67.6 %all-gather.1 = f32[32,24,2]{1,2,0:T(2,128)S(1)} all-gather(f32[1,24,2]{1,2,0:T(2,128)S(1)} %bitcast.196), channel_id=1, replica_groups=mesh['dp'=8,'tensor'=4] {'dp','tensor'}, dimensions={0}, use_global_device_ids=true | all-gather | bytes 6336 | tf_op jit(solution)/shard_map/all_gather | solution.py:121
  355.4 1.3 fusion.83
  356.8 12.5 %all-reduce.4 = f32[3,3,64]{2,1,0:T(4,128)S(1)} all-reduce(f32[3,3,64]{2,1,0:T(4,128)S(1)} %fusion.83), channel_id=7, replica_groups=mesh['dp'=8,'tensor'=4] {'dp'}, use_global_device_ids=true, to_apply=%region_19.20.clone | all-reduce | flops 576 | bytes 4608
  370.0 1.4 copy.58
  371.3 1.6 copy.56
  373.0 12.4 %reduce-scatter.16.cloned.1.call-done = f32[1,256,768]{2,1,0:T(8,128)} async-done(((f32[1,1024,768]{2,1,0:T(8,128)}), f32[1,256,768]{2,1,0:T(8,128)}) %reduce-scatter.16.cloned.1.call-update) | async-done | bytes 786448 | tf_op jit(solution)/shard_map/reduce_scatter | solution.py:214
  385.4 1.6 fusion.116
  386.9 61.0 %reduce-scatter.14.cloned.1.call-done = f32[1,256,768]{2,1,0:T(8,128)} async-done(((f32[1,1024,768]{2,1,0:T(8,128)}), f32[1,256,768]{2,1,0:T(8,128)}) %reduce-scatter.14.cloned.1.call-update) | async-done | bytes 786448 | tf_op jit(solution)/shard_map/reduce_scatter | solution.py:164
  448.0 2.6 convert_reduce_fusion.1
  450.6 40.4 %all-reduce.6 = (f32[768]{0:T(1024)S(1)}, f32[768]{0:T(1024)S(1)}, f32[2,768]{1,0:T(2,128)S(1)}) all-reduce(f32[768]{0:T(1024)S(1)} %get-tuple-element.186, f32[768]{0:T(1024)S(1)} %get-tuple-element.189, f32[2,768]{1,0:T(2,128)S(1)} %pad_maximum_fusion.3), channel_id=4, replica_groups=mesh['dp'=8,'tensor'=4] {'dp','tensor'}, use_global_device_ids=true, to_apply=%region_14.15.clone | all-reduce | flops 3072 | bytes 24576
  492.8 1.5 reduce-scatter.18.cloned.1.call-done
  494.3 46.2 %reduce-scatter.20.cloned.1.call-done = f32[96,768]{1,0:T(8,128)} async-done(((f32[768,768]{1,0:T(8,128)}), f32[96,768]{1,0:T(8,128)}) %reduce-scatter.20.cloned.1.call-update) | async-done | bytes 294928 | tf_op jit(solution)/shard_map/reduce_scatter | solution.py:238
  540.5 46.3 %reduce-scatter.22.cloned.1.call-done = f32[768,96]{0,1:T(8,128)} async-done(((f32[768,768]{0,1:T(8,128)}), f32[768,96]{0,1:T(8,128)}) %reduce-scatter.22.cloned.1.call-update) | async-done | bytes 294928 | tf_op jit(solution)/shard_map/reduce_scatter | solution.py:240
  (145 shorter events, 18.0 us)
Async XLA Ops:
  7.2 93.4 %all-gather.7.cloned.1.call-start = ((), (), s32[]{:S(2)}) async-start(), calls=%async_computation.7 | async-start | bytes 1966080 | tf_op jit(solution)/shard_map/all_gather | solution.py:142
  8.4 49.3 %copy-start.17 = (f32[256]{0:T(256)}, f32[256]{0:T(256)S(1)}, u32[]{:S(2)}) copy-start(f32[256]{0:T(256)S(1)} %broadcast_multiply_fusion.3) | copy-start | bytes 3076
  9.6 48.0 %copy-start.19 = (f32[256]{0:T(256)}, f32[256]{0:T(256)S(1)}, u32[]{:S(2)}) copy-start(f32[256]{0:T(256)S(1)} %add_rsqrt_fusion) | copy-start | bytes 3076
  53.4 4.3 copy-start.15
  53.4 19.0 %copy-start.21 = (bf16[3,3,8]{2,1,0:T(4,128)(2,1)S(1)}, bf16[3,3,8]{2,1,0:T(4,128)(2,1)}, u32[]{:S(2)}) copy-start(bf16[3,3,8]{2,1,0:T(4,128)(2,1)} %param.19) | copy-start | bytes 436
  53.4 28.6 %copy-start.14 = (bf16[192,96]{1,0:T(8,128)(2,1)S(1)}, bf16[192,96]{1,0:T(8,128)(2,1)}, u32[]{:S(2)}) copy-start(bf16[192,96]{1,0:T(8,128)(2,1)} %param.20) | copy-start | bytes 110596
  55.4 35.2 %copy-start.22 = (bf16[6,16]{1,0:T(8,128)(2,1)S(1)}, bf16[6,16]{1,0:T(8,128)(2,1)}, u32[]{:S(2)}) copy-start(bf16[6,16]{1,0:T(8,128)(2,1)} %param.22) | copy-start | bytes 580
  55.4 74.4 %all-gather.13.cloned.1.call-start = ((), (), s32[]{:S(2)}) async-start(), calls=%async_computation.11 | async-start | bytes 1966080 | tf_op jit(solution)/shard_map/all_gather | solution.py:168
  56.2 184.3 %all-gather.9.cloned.1.call-start = ((), (), s32[]{:S(2)}) async-start(), calls=%async_computation.8 | async-start | bytes 1327104 | tf_op jit(solution)/shard_map/all_gather | solution.py:127
  56.9 189.0 %all-gather.11.cloned.1.call-start = ((), (), s32[]{:S(2)}) async-start(), calls=%async_computation.9 | async-start | bytes 1327104 | tf_op jit(solution)/shard_map/all_gather | solution.py:129
  57.5 312.5 %reduce-scatter.26.cloned.1.call-start = ((), (), s32[]{:S(2)}) async-start(), calls=%async_computation.17 | async-start | bytes 73728
  72.4 30.8 %copy-start.8 = (bf16[768,3,192]{0,2,1:T(8,128)(2,1)}, bf16[768,3,192]{0,2,1:T(8,128)(2,1)S(1)}, u32[]{:S(2)}) copy-start(bf16[768,3,192]{0,2,1:T(8,128)(2,1)S(1)} %copy.41) | copy-start | bytes 2654212
  100.5 3.0 copy-start.11
  122.0 10.0 %copy-start.10 = (bf16[2,512,3,64]{1,3,2,0:T(8,128)(2,1)}, bf16[2,512,3,64]{1,3,2,0:T(8,128)(2,1)S(1)}, u32[]{:S(2)}) copy-start(bf16[2,512,3,64]{1,3,2,0:T(8,128)(2,1)S(1)} %get-tuple-element.148) | copy-start | bytes 1179652
  164.6 14.4 %copy-start.4 = (f32[1024,3,64]{0,2,1:T(8,128)S(1)}, f32[1024,3,64]{0,2,1:T(8,128)}, u32[]{:S(2)}) copy-start(f32[1024,3,64]{0,2,1:T(8,128)} %get-tuple-element.416) | copy-start | bytes 2359300 | tf_op jit(solution)/shard_map/while/body/eval_jaxpr/while
  183.7 0.9 copy-start.5
  216.8 14.6 %copy-start.4 = (f32[1024,3,64]{0,2,1:T(8,128)S(1)}, f32[1024,3,64]{0,2,1:T(8,128)}, u32[]{:S(2)}) copy-start(f32[1024,3,64]{0,2,1:T(8,128)} %get-tuple-element.416) | copy-start | bytes 2359300 | tf_op jit(solution)/shard_map/while/body/eval_jaxpr/while
  236.1 0.9 copy-start.5
  240.4 11.3 %copy-start.2 = (bf16[24,8,2,512]{3,1,2,0:T(8,128)(2,1)}, bf16[24,8,2,512]{3,1,2,0:T(8,128)(2,1)S(1)}, u32[]{:S(2)}) copy-start(bf16[24,8,2,512]{3,1,2,0:T(8,128)(2,1)S(1)} %copy.72) | copy-start | bytes 1179652
  240.5 5.5 copy-start.1
  246.0 7.4 %copy-start.12 = (f32[1024,8]{0,1:T(8,128)S(1)}, f32[1024,8]{0,1:T(8,128)}, u32[]{:S(2)}) copy-start(f32[1024,8]{0,1:T(8,128)} %copy-done.11) | copy-start | bytes 98308
  246.0 7.4 %copy-start.13 = (f32[1024,8]{0,1:T(8,128)S(1)}, f32[1024,8]{0,1:T(8,128)}, u32[]{:S(2)}) copy-start(f32[1024,8]{0,1:T(8,128)} %get-tuple-element.250) | copy-start | bytes 98308
  251.7 119.6 %reduce-scatter.24.cloned.1.call-start = ((), (), s32[]{:S(2)}) async-start(), calls=%async_computation.16 | async-start | bytes 884736
  257.9 127.5 %reduce-scatter.16.cloned.1.call-start = ((), (), s32[]{:S(2)}) async-start(), calls=%async_computation.12 | async-start | bytes 3932160 | tf_op jit(solution)/shard_map/reduce_scatter | solution.py:214
  257.9 3.9 copy-start.24
  257.9 3.9 copy-start.26
  261.8 1.5 copy-start.7
  261.8 1.6 copy-start.9
  266.6 181.4 %reduce-scatter.14.cloned.1.call-start = ((), (), s32[]{:S(2)}) async-start(), calls=%async_computation.10 | async-start | bytes 3932160 | tf_op jit(solution)/shard_map/reduce_scatter | solution.py:164
  266.6 3.2 copy-start.3
  272.3 222.1 %reduce-scatter.18.cloned.1.call-start = ((), (), s32[]{:S(2)}) async-start(), calls=%async_computation.13 | async-start | bytes 2654208 | tf_op jit(solution)/shard_map/reduce_scatter | solution.py:235
  276.9 263.6 %reduce-scatter.20.cloned.1.call-start = ((), (), s32[]{:S(2)}) async-start(), calls=%async_computation.14 | async-start | bytes 2654208 | tf_op jit(solution)/shard_map/reduce_scatter | solution.py:238
  282.0 4.5 copy-start.23
  282.0 72.1 %copy-start.25 = (u32[32]{0:T(128)S(1)}, u32[32]{0:T(128)}, u32[]{:S(2)}) copy-start(u32[32]{0:T(128)} %constant.134) | copy-start | bytes 388
  282.1 304.8 %reduce-scatter.22.cloned.1.call-start = ((), (), s32[]{:S(2)}) async-start(), calls=%async_computation.15 | async-start | bytes 2654208 | tf_op jit(solution)/shard_map/reduce_scatter | solution.py:240
  286.4 98.9 %copy-start = (bf16[1,256,768]{2,1,0:T(8,128)(2,1)S(1)}, bf16[1,256,768]{2,1,0:T(8,128)(2,1)}, u32[]{:S(2)}) copy-start(bf16[1,256,768]{2,1,0:T(8,128)(2,1)} %param.15) | copy-start | bytes 1179652
  286.4 98.9 %copy-start.16 = (f32[768]{0:T(1024)S(1)}, f32[768]{0:T(1024)}, u32[]{:S(2)}) copy-start(f32[768]{0:T(1024)} %copy-done.15) | copy-start | bytes 9220
  286.5 98.9 %copy-start.18 = (f32[256]{0:T(256)S(1)}, f32[256]{0:T(256)}, u32[]{:S(2)}) copy-start(f32[256]{0:T(256)} %copy-done.17) | copy-start | bytes 3076
  286.5 98.9 %copy-start.20 = (f32[256]{0:T(256)S(1)}, f32[256]{0:T(256)}, u32[]{:S(2)}) copy-start(f32[256]{0:T(256)} %copy-done.19) | copy-start | bytes 3076
  286.5 161.5 %copy-start.6 = (bf16[1,256,768]{2,1,0:T(8,128)(2,1)S(1)}, bf16[1,256,768]{2,1,0:T(8,128)(2,1)}, u32[]{:S(2)}) copy-start(bf16[1,256,768]{2,1,0:T(8,128)(2,1)} %param.25) | copy-start | bytes 1179652
Sparse Core Ops, SparseCore 0:
  55.6 36.8 all-gather.6
  94.0 35.8 all-gather.12
  131.8 22.8 all-gather.8
  156.4 23.9 all-gather.10
  251.8 32.6 reduce-scatter.25
  287.5 34.9 reduce-scatter.23
  324.8 60.5 reduce-scatter.15
  387.6 60.2 reduce-scatter.13
  451.9 42.4 reduce-scatter.17
  498.1 42.3 reduce-scatter.19
  544.5 42.3 reduce-scatter.21
where the time goes:
time: 603 us; the launch traced here: 594 us
  blocking collectives  202 us (33%)
  waiting for transfers between devices  177 us (29%)
  matrix products  127 us (21%)
  local copies, waits for them, and re-layouts  38.7 us (6%)
  other arithmetic  22.8 us (4%)
  between operations  15.3 us (3%)
  loops' own time  9.92 us (2%)
    unnamed x3, blocking collectives  95 us
    all_gather x1, blocking collectives, body(): lax.all_gather(out_bias, ('dp', 'tensor'), axis=1, tiled=True)  67.6 us
    reduce_scatter x1, waiting for transfers between devices, body(): lax.psum_scatter(branch.reshape(seqs, length, model), 'tensor', scatter_d...  61 us
    reduce_scatter x1, waiting for transfers between devices, body(): lax.psum_scatter(grad_down, 'dp', scatter_dimension=1, tiled=True)  46.3 us
    reduce_scatter x1, waiting for transfers between devices, body(): lax.psum_scatter(grad_in, 'dp', scatter_dimension=0, tiled=True)  46.2 us
    dot_general x2, matrix products, one_block(): jnp.einsum('hqk,qhd->khd', score_grad, q_rows, preferred_element_type=jnp...  29 us
    dot_general x2, matrix products, one_block(): jnp.einsum('hqk,khd->qhd', score_grad, key_rows, preferred_element_type=j...  25.4 us
    dynamic_update_slice x4, local copies, waits for them, and re-layouts, attend_back(): lax.scan(one_block, (zero_grads, zero_grads), jnp.arange(length // block_...  17 us
  transfers between devices with their start and end apart: 11, of which 6 were waited for; matrix products, arithmetic and copies ran while one was open for 29% of the time, Pallas kernels for 0%

commit v1 on v0

--- a/solution.py
+++ b/solution.py
@@ -9,6 +9,28 @@
 ROOT_HALF = 0.7071067811865476
 INV_ROOT_TAU = 0.3989422804014327
 NEG_BIG = -1e30
+
+
+def _draw_run(load, on_dim):
+    raw_out = list(load.shape[1:])
+    raw_out[on_dim] *= load.shape[0]
+    return jnp.moveaxis(load, 0, on_dim).reshape(raw_out)
+
+
+def fit_pieces_all_for(work_x, chip_axis):
+    n_blocks = lax.axis_size(chip_axis)
+    q_next = work_x[None]
+    for d in range(n_blocks.bit_length() - 1):
+        small = 1 << d
+        later = lax.ppermute(q_next, chip_axis, [(nth, nth ^ small) for nth in range(n_blocks)])
+        v_next = jnp.stack([q_next, later], axis=0)
+        known = lax.axis_index(chip_axis) >> d & 1
+        q_next = jnp.where(known == 0, v_next, v_next[::-1]).reshape(-1, *work_x.shape)
+    return q_next
+
+
+def outputs_work(local_block, matrix, d_out):
+    return _draw_run(fit_pieces_all_for(local_block, matrix), d_out)
 
 
 def rotary_tables(length, rot_dims):
@@ -118,7 +140,7 @@
     gain, shift, biases = (
         lax.all_gather(ln_gain, ("dp", "tensor"), axis=0, tiled=True),
         lax.all_gather(ln_bias, ("dp", "tensor"), axis=0, tiled=True),
-        lax.all_gather(out_bias, ("dp", "tensor"), axis=1, tiled=True),
+        outputs_work(out_bias, ("dp", "tensor"), 1),
     )
     forward_weights = (
         lax.all_gather(w_qkv, "dp", axis=0, tiled=True),

time: 603 us -> 603 us (level)
  blocking collectives: 202 us -> 134 us
  waiting for transfers between devices: 177 us -> 241 us
    all_gather x1 -> x0, blocking collectives: 67.6 us -> none  [body(): lax.all_gather(out_bias, ('dp', 'tensor'), axis=1, tiled=True)]
    reduce_scatter x1, waiting for transfers between devices: 12.4 us -> 61.1 us  [body(): lax.psum_scatter(norm_grad.reshape(seqs, length, model), 'tensor', scatte...]
    ppermute x0 -> x5, waiting for transfers between devices: none -> 10.1 us  [fit_pieces_all_for(): lax.ppermute(q_next, chip_axis, [(nth, nth ^ small) for nth in range(n_bl...]
  transfers between devices with their start and end apart: 11 -> 16, of which waited for: 6 -> 12; matrix products, arithmetic and copies ran while one was open for 29% -> 29% of each run, Pallas kernels for 0% -> 0%
where the time goes in v1:
time: 603 us; the launch traced here: 593 us
  waiting for transfers between devices  241 us (40%)
  blocking collectives  134 us (22%)
  matrix products  127 us (21%)
  local copies, waits for them, and re-layouts  38.6 us (6%)
  other arithmetic  21.7 us (4%)
  between operations  15.4 us (3%)
  loops' own time  9.92 us (2%)
  starting transfers between devices  6.24 us (1%)
    unnamed x3, blocking collectives  94.6 us
    reduce_scatter x1, waiting for transfers between devices, body(): lax.psum_scatter(norm_grad.reshape(seqs, length, model), 'tensor', scatte...  61.1 us
    reduce_scatter x1, waiting for transfers between devices, body(): lax.psum_scatter(branch.reshape(seqs, length, model), 'tensor', scatter_d...  61 us
    reduce_scatter x1, waiting for transfers between devices, body(): lax.psum_scatter(grad_down, 'dp', scatter_dimension=1, tiled=True)  46.3 us
    reduce_scatter x1, waiting for transfers between devices, body(): lax.psum_scatter(grad_in, 'dp', scatter_dimension=0, tiled=True)  46.2 us
    dot_general x2, matrix products, one_block(): jnp.einsum('hqk,qhd->khd', score_grad, q_rows, preferred_element_type=jnp...  29 us
    dot_general x2, matrix products, one_block(): jnp.einsum('hqk,khd->qhd', score_grad, key_rows, preferred_element_type=j...  25.4 us
    dynamic_update_slice x4, local copies, waits for them, and re-layouts, attend_back(): lax.scan(one_block, (zero_grads, zero_grads), jnp.arange(length // block_...  16.9 us
  transfers between devices with their start and end apart: 16, of which 12 were waited for; matrix products, arithmetic and copies ran while one was open for 29% of the time, Pallas kernels for 0%

profile of v1, /device:TPU:0, one launch (start us, length us, event | category | flops | bytes accessed | tf_op | source)
XLA Modules:
  0.0 593.4 jit_solution(8830012395577200691)
XLA Ops:
  8.4 1.2 fusion.117
  11.3 42.0 %all-reduce.7 = (f32[768]{0:T(1024)S(1)}, f32[768]{0:T(1024)S(1)}) all-reduce(f32[768]{0:T(1024)S(1)} %dynamic-update-slice.1, f32[768]{0:T(1024)S(1)} %dynamic-update-slice), channel_id=1, replica_groups=mesh['dp'=8,'tensor'=4] {'dp','tensor'}, use_global_device_ids=true, to_apply=%add.1 | all-reduce | flops 1536 | bytes 12288
  53.4 2.0 fusion.112
  58.7 12.8 %all_gather.37 = bf16[768,3,192]{2,1,0:T(4,128)(2,1)S(1)} all-gather(bf16[96,3,192]{2,1,0:T(4,128)(2,1)S(1)} %copy.42), channel_id=1, replica_groups=mesh['dp'=8,'tensor'=4] {'dp'}, dimensions={0}, use_global_device_ids=true | all-gather | bytes 995328 | tf_op jit(solution)/shard_map/all_gather | solution.py:146
  72.5 9.4 %all_gather.38 = bf16[3,3,64]{1,0,2:T(4,128)(2,1)S(1)} all-gather(bf16[3,3,8]{1,0,2:T(4,128)(2,1)S(1)} %copy.44), channel_id=1, replica_groups=mesh['dp'=8,'tensor'=4] {'dp'}, dimensions={2}, use_global_device_ids=true | all-gather | bytes 1296 | tf_op jit(solution)/shard_map/all_gather | solution.py:147
  82.1 8.4 %all_gather.39 = bf16[192,768]{0,1:T(8,128)(2,1)S(1)} all-gather(bf16[192,96]{0,1:T(8,128)(2,1)S(1)} %copy.47), channel_id=1, replica_groups=mesh['dp'=8,'tensor'=4] {'dp'}, dimensions={1}, use_global_device_ids=true | all-gather | bytes 331776 | tf_op jit(solution)/shard_map/all_gather | solution.py:148
  90.6 9.0 %all-gather = bf16[8,16,6]{1,2,0:T(8,128)(2,1)S(1)} all-gather(bf16[1,16,6]{1,2,0:T(8,128)(2,1)S(1)} %bitcast.221), channel_id=1, replica_groups=mesh['dp'=8,'tensor'=4] {'dp'}, dimensions={0}, use_global_device_ids=true | all-gather | bytes 1728 | tf_op jit(solution)/shard_map/all_gather | solution.py:150
  100.5 2.7 add_bitcast_fusion.2
  103.7 18.3 %while.47 = (s32[]{:T(128)}, bf16[2,512,3,64]{1,3,2,0:T(8,128)(2,1)S(1)}, f32[2,3,512]{2,1,0:T(4,128)S(1)}, s32[2]{0:T(128)S(1)}, bf16[1024,3,64]{0,2,1:T(8,128)...) while((s32[]{:T(128)}, ...), condition=%wide.region_5.6_spmd, body=%wide.region_2.5_spmd.sunk | while | flops 422149120 | bytes 22214820 | solution.py:96
  107.2 1.5 fusion.180
  108.8 1.8 fusion.181
  110.6 2.2 fusion.182
  116.4 1.5 fusion.180
  117.9 1.8 fusion.181
  119.8 2.2 fusion.182
  122.0 7.9 %all-gather.12.cloned.1.call-done = bf16[1,1024,768]{2,1,0:T(8,128)(2,1)} async-done(((bf16[1,256,768]{2,1,0:T(8,128)(2,1)}), bf16[1,1024,768]{2,1,0:T(8,128)(2,1)}) %all-gather.12.cloned.1.call-update) | async-done | bytes 1572880 | tf_op jit(solution)/shard_map/all_gather | solution.py:190
  129.9 2.1 fusion.102
  132.0 105.0 %while.48 = (s32[]{:T(128)}, f32[1024,3,64]{0,2,1:T(8,128)}, f32[1024,3,64]{0,2,1:T(8,128)}, f32[2,512,3,64]{1,0,3,2:T(2,128)}, s32[2]{0:T(128)S(1)}, /*index=5*...) while((s32[]{:T(128)}, f32[1024,3,64]{0,2,1:T(8,128)}, ...), condition=%wide.region_9.10_spmd.clone, body=%wide.region_7.9_spmd.clone.sunk | while | flops 1048843776 | bytes 72661312 | solution.py:133
  133.7 3.7 fusion.194
  137.4 3.7 fusion.193
  143.4 12.7 %fusion.197 = f32[1,512,3,64]{1,3,2,0:T(8,128)S(1)} fusion(bf16[1024,3,64]{0,2,1:T(8,128)(2,1)S(1)} %get-tuple-element.439, f32[3,512,1024]{2,1,0:T(8,128)} %fusion.193, f32[3,512,1024]{2,1,0:T(8,128)} %fusion.194, f32[3,512]{1,0:T(4,128)S(1)} %dynamic-slice_bitcast_fusion.2, pred[512,1024]{1,0:T(8,128)(4,1)S(1)} %iota_compare_fusion.5), kind=kOutput, calls=%fused_computation.40.clone.1 | convolution fusion | flops 218630656 | bytes 13899776 | tf_op jit(solution)/shard_map/while/body/eval_jaxpr/while/body/eval_jaxpr/hqk,khd->qhd/dot_general | solution.py:124
  156.5 8.1 %dynamic_update_slice.33 = f32[2,512,3,64]{1,0,3,2:T(2,128)} dynamic-update-slice(f32[2,512,3,64]{1,0,3,2:T(2,128)} %get-tuple-element.421, f32[1,512,3,64]{1,0,3,2:T(1,128)S(1)} %copy.81, s32[]{:T(128)} %get-tuple-element.418, s32[]{:T(128)} %constant.71.clone.1..sunk.1, s32[]{:T(128)} %constant.71.clone.1..sunk.1, s32[]{:T(128)} %constant.71.clone.1..sunk.1) | dynamic-update-slice | bytes 786436 | tf_op jit(solution)/shard_map/while/body/eval_jaxpr/while/body/jit(dynamic_update_index_in_dim)/dynamic_update_slice | solution.py:133
  164.5 14.4 %fusion.195 = f32[1024,3,64]{0,2,1:T(8,128)} fusion(f32[3,512,1024]{2,1,0:T(8,128)} %fusion.193, f32[3,512,1024]{2,1,0:T(8,128)} %fusion.194, f32[3,512]{1,0:T(4,128)S(1)} %dynamic-slice_bitcast_fusion.2, pred[512,1024]{1,0:T(8,128)(4,1)S(1)} %iota_compare_fusion.5, f32[1024,3,64]{0,2,1:T(8,128)} %get-tuple-element.419, pred[]{:T(512)S(6)} %compare.3, ...), kind=kOutput, calls=%fused_computation.38.clone.1 | convolution fusion | flops 219023872 | bytes 28000260 | tf_op jit(solution)/shard_map/while/body/eval_jaxpr/while/body/eval_jaxpr/hqk,qhd->khd/dot_general | solution.py:127
  179.0 4.7 fusion.196
  185.8 3.7 fusion.194
  189.5 3.7 fusion.193
  195.5 12.7 %fusion.197 = f32[1,512,3,64]{1,3,2,0:T(8,128)S(1)} fusion(bf16[1024,3,64]{0,2,1:T(8,128)(2,1)S(1)} %get-tuple-element.439, f32[3,512,1024]{2,1,0:T(8,128)} %fusion.193, f32[3,512,1024]{2,1,0:T(8,128)} %fusion.194, f32[3,512]{1,0:T(4,128)S(1)} %dynamic-slice_bitcast_fusion.2, pred[512,1024]{1,0:T(8,128)(4,1)S(1)} %iota_compare_fusion.5), kind=kOutput, calls=%fused_computation.40.clone.1 | convolution fusion | flops 218630656 | bytes 13899776 | tf_op jit(solution)/shard_map/while/body/eval_jaxpr/while/body/eval_jaxpr/hqk,khd->qhd/dot_general | solution.py:124
  208.6 8.0 %dynamic_update_slice.33 = f32[2,512,3,64]{1,0,3,2:T(2,128)} dynamic-update-slice(f32[2,512,3,64]{1,0,3,2:T(2,128)} %get-tuple-element.421, f32[1,512,3,64]{1,0,3,2:T(1,128)S(1)} %copy.81, s32[]{:T(128)} %get-tuple-element.418, s32[]{:T(128)} %constant.71.clone.1..sunk.1, s32[]{:T(128)} %constant.71.clone.1..sunk.1, s32[]{:T(128)} %constant.71.clone.1..sunk.1) | dynamic-update-slice | bytes 786436 | tf_op jit(solution)/shard_map/while/body/eval_jaxpr/while/body/jit(dynamic_update_index_in_dim)/dynamic_update_slice | solution.py:133
  216.7 14.6 %fusion.195 = f32[1024,3,64]{0,2,1:T(8,128)} fusion(f32[3,512,1024]{2,1,0:T(8,128)} %fusion.193, f32[3,512,1024]{2,1,0:T(8,128)} %fusion.194, f32[3,512]{1,0:T(4,128)S(1)} %dynamic-slice_bitcast_fusion.2, pred[512,1024]{1,0:T(8,128)(4,1)S(1)} %iota_compare_fusion.5, f32[1024,3,64]{0,2,1:T(8,128)} %get-tuple-element.419, pred[]{:T(512)S(6)} %compare.3, ...), kind=kOutput, calls=%fused_computation.38.clone.1 | convolution fusion | flops 219023872 | bytes 28000260 | tf_op jit(solution)/shard_map/while/body/eval_jaxpr/while/body/eval_jaxpr/hqk,qhd->khd/dot_general | solution.py:127
  231.2 4.7 fusion.196
  237.0 1.8 broadcast_in_dim.78
  238.8 1.4 copy.46
  240.3 5.5 multiply_convert_fusion.1
  245.8 4.9 fusion.135
  251.6 1.6 fusion.99
  253.2 1.7 multiply_subtract_fusion.1
  255.7 1.9 slice.89
  257.8 1.3 maximum_bitcast_fusion
  260.2 1.4 fusion.84
  261.6 1.4 fusion.123
  263.2 3.1 add_bitcast_fusion
  266.4 3.2 fusion.136
  269.7 2.3 add_bitcast_fusion.1
  272.1 4.7 fusion.85
  277.0 4.8 fusion.97
  281.9 4.3 fusion.88
  287.1 2.8 collective-permute-done
  290.0 1.5 collective-permute-start.1
  291.5 3.0 collective-permute-done.1
  295.8 1.6 collective-permute-start.3
  297.4 2.1 collective-permute-done.3
  299.5 1.6 collective-permute-start.4
  303.7 12.1 %all-reduce.4 = f32[3,3,64]{2,1,0:T(4,128)S(1)} all-reduce(f32[3,3,64]{2,1,0:T(4,128)S(1)} %fusion.83), channel_id=7, replica_groups=mesh['dp'=8,'tensor'=4] {'dp'}, use_global_device_ids=true, to_apply=%region_19.20.clone | all-reduce | flops 576 | bytes 4608
  316.6 1.4 copy.61
  317.9 4.5 reduce-scatter.24.cloned.1.call-done
  322.4 1.6 copy.59
  324.0 61.1 %reduce-scatter.16.cloned.1.call-done = f32[1,256,768]{2,1,0:T(8,128)} async-done(((f32[1,1024,768]{2,1,0:T(8,128)}), f32[1,256,768]{2,1,0:T(8,128)}) %reduce-scatter.16.cloned.1.call-update) | async-done | bytes 786448 | tf_op jit(solution)/shard_map/reduce_scatter | solution.py:236
  385.1 1.6 fusion.116
  386.7 61.0 %reduce-scatter.14.cloned.1.call-done = f32[1,256,768]{2,1,0:T(8,128)} async-done(((f32[1,1024,768]{2,1,0:T(8,128)}), f32[1,256,768]{2,1,0:T(8,128)}) %reduce-scatter.14.cloned.1.call-update) | async-done | bytes 786448 | tf_op jit(solution)/shard_map/reduce_scatter | solution.py:186
  447.8 2.6 convert_reduce_fusion.1
  450.4 40.4 %all-reduce.6 = (f32[768]{0:T(1024)S(1)}, f32[768]{0:T(1024)S(1)}, f32[2,768]{1,0:T(2,128)S(1)}) all-reduce(f32[768]{0:T(1024)S(1)} %get-tuple-element.186, f32[768]{0:T(1024)S(1)} %get-tuple-element.189, f32[2,768]{1,0:T(2,128)S(1)} %pad_maximum_fusion.6), channel_id=4, replica_groups=mesh['dp'=8,'tensor'=4] {'dp','tensor'}, use_global_device_ids=true, to_apply=%region_14.15.clone | all-reduce | flops 3072 | bytes 24576
  492.6 1.5 reduce-scatter.18.cloned.1.call-done
  494.1 46.2 %reduce-scatter.20.cloned.1.call-done = f32[96,768]{1,0:T(8,128)} async-done(((f32[768,768]{1,0:T(8,128)}), f32[96,768]{1,0:T(8,128)}) %reduce-scatter.20.cloned.1.call-update) | async-done | bytes 294928 | tf_op jit(solution)/shard_map/reduce_scatter | solution.py:260
  540.4 46.3 %reduce-scatter.22.cloned.1.call-done = f32[768,96]{0,1:T(8,128)} async-done(((f32[768,768]{0,1:T(8,128)}), f32[768,96]{0,1:T(8,128)}) %reduce-scatter.22.cloned.1.call-update) | async-done | bytes 294928 | tf_op jit(solution)/shard_map/reduce_scatter | solution.py:262
  (167 shorter events, 26.5 us)
Async XLA Ops:
  7.2 93.4 %all-gather.6.cloned.1.call-start = ((), (), s32[]{:S(2)}) async-start(), calls=%async_computation.7 | async-start | bytes 1966080 | tf_op jit(solution)/shard_map/all_gather | solution.py:164
  8.4 49.3 %copy-start.18 = (f32[256]{0:T(256)}, f32[256]{0:T(256)S(1)}, u32[]{:S(2)}) copy-start(f32[256]{0:T(256)S(1)} %broadcast_multiply_fusion.3) | copy-start | bytes 3076
  9.6 48.0 %copy-start.20 = (f32[256]{0:T(256)}, f32[256]{0:T(256)S(1)}, u32[]{:S(2)}) copy-start(f32[256]{0:T(256)S(1)} %add_rsqrt_fusion) | copy-start | bytes 3076
  53.4 4.3 copy-start.16
  53.4 19.0 %copy-start.22 = (bf16[3,3,8]{2,1,0:T(4,128)(2,1)S(1)}, bf16[3,3,8]{2,1,0:T(4,128)(2,1)}, u32[]{:S(2)}) copy-start(bf16[3,3,8]{2,1,0:T(4,128)(2,1)} %param.19) | copy-start | bytes 436
  53.4 28.6 %copy-start.15 = (bf16[192,96]{1,0:T(8,128)(2,1)S(1)}, bf16[192,96]{1,0:T(8,128)(2,1)}, u32[]{:S(2)}) copy-start(bf16[192,96]{1,0:T(8,128)(2,1)} %param.20) | copy-start | bytes 110596
  55.4 35.2 %copy-start.23 = (bf16[6,16]{1,0:T(8,128)(2,1)S(1)}, bf16[6,16]{1,0:T(8,128)(2,1)}, u32[]{:S(2)}) copy-start(bf16[6,16]{1,0:T(8,128)(2,1)} %param.22) | copy-start | bytes 580
  55.4 74.4 %all-gather.12.cloned.1.call-start = ((), (), s32[]{:S(2)}) async-start(), calls=%async_computation.11 | async-start | bytes 1966080 | tf_op jit(solution)/shard_map/all_gather | solution.py:190
  56.2 184.1 %all-gather.8.cloned.1.call-start = ((), (), s32[]{:S(2)}) async-start(), calls=%async_computation.8 | async-start | bytes 1327104 | tf_op jit(solution)/shard_map/all_gather | solution.py:149
  56.9 188.9 %all-gather.10.cloned.1.call-start = ((), (), s32[]{:S(2)}) async-start(), calls=%async_computation.9 | async-start | bytes 1327104 | tf_op jit(solution)/shard_map/all_gather | solution.py:151
  57.5 259.1 %reduce-scatter.26.cloned.1.call-start = ((), (), s32[]{:S(2)}) async-start(), calls=%async_computation.17 | async-start | bytes 73728
  72.4 30.8 %copy-start.9 = (bf16[768,3,192]{0,2,1:T(8,128)(2,1)}, bf16[768,3,192]{0,2,1:T(8,128)(2,1)S(1)}, u32[]{:S(2)}) copy-start(bf16[768,3,192]{0,2,1:T(8,128)(2,1)S(1)} %copy.43) | copy-start | bytes 2654212
  100.5 3.0 copy-start.12
  122.0 10.0 %copy-start.11 = (bf16[2,512,3,64]{1,3,2,0:T(8,128)(2,1)}, bf16[2,512,3,64]{1,3,2,0:T(8,128)(2,1)S(1)}, u32[]{:S(2)}) copy-start(bf16[2,512,3,64]{1,3,2,0:T(8,128)(2,1)S(1)} %get-tuple-element.148) | copy-start | bytes 1179652
  164.5 14.4 %copy-start.4 = (f32[1024,3,64]{0,2,1:T(8,128)S(1)}, f32[1024,3,64]{0,2,1:T(8,128)}, u32[]{:S(2)}) copy-start(f32[1024,3,64]{0,2,1:T(8,128)} %get-tuple-element.420) | copy-start | bytes 2359300 | tf_op jit(solution)/shard_map/while/body/eval_jaxpr/while
  183.7 0.9 copy-start.5
  216.7 14.6 %copy-start.4 = (f32[1024,3,64]{0,2,1:T(8,128)S(1)}, f32[1024,3,64]{0,2,1:T(8,128)}, u32[]{:S(2)}) copy-start(f32[1024,3,64]{0,2,1:T(8,128)} %get-tuple-element.420) | copy-start | bytes 2359300 | tf_op jit(solution)/shard_map/while/body/eval_jaxpr/while
  235.9 0.9 copy-start.5
  240.2 11.3 %copy-start.2 = (bf16[24,8,2,512]{3,1,2,0:T(8,128)(2,1)}, bf16[24,8,2,512]{3,1,2,0:T(8,128)(2,1)S(1)}, u32[]{:S(2)}) copy-start(bf16[24,8,2,512]{3,1,2,0:T(8,128)(2,1)S(1)} %copy.75) | copy-start | bytes 1179652
  240.3 5.5 copy-start.1
  245.8 7.4 %copy-start.13 = (f32[1024,8]{0,1:T(8,128)S(1)}, f32[1024,8]{0,1:T(8,128)}, u32[]{:S(2)}) copy-start(f32[1024,8]{0,1:T(8,128)} %copy-done.12) | copy-start | bytes 98308
  245.8 7.4 %copy-start.14 = (f32[1024,8]{0,1:T(8,128)S(1)}, f32[1024,8]{0,1:T(8,128)}, u32[]{:S(2)}) copy-start(f32[1024,8]{0,1:T(8,128)} %get-tuple-element.252) | copy-start | bytes 98308
  251.5 70.9 %reduce-scatter.24.cloned.1.call-start = ((), (), s32[]{:S(2)}) async-start(), calls=%async_computation.16 | async-start | bytes 884736
  257.7 127.4 %reduce-scatter.16.cloned.1.call-start = ((), (), s32[]{:S(2)}) async-start(), calls=%async_computation.12 | async-start | bytes 3932160 | tf_op jit(solution)/shard_map/reduce_scatter | solution.py:236
  257.7 3.9 copy-start.25
  257.8 3.9 copy-start.27
  261.6 1.5 copy-start.8
  261.6 1.6 copy-start.10
  266.4 181.4 %reduce-scatter.14.cloned.1.call-start = ((), (), s32[]{:S(2)}) async-start(), calls=%async_computation.10 | async-start | bytes 3932160 | tf_op jit(solution)/shard_map/reduce_scatter | solution.py:186
  266.4 3.2 copy-start.3
  272.0 222.1 %reduce-scatter.18.cloned.1.call-start = ((), (), s32[]{:S(2)}) async-start(), calls=%async_computation.13 | async-start | bytes 2654208 | tf_op jit(solution)/shard_map/reduce_scatter | solution.py:257
  276.7 263.6 %reduce-scatter.20.cloned.1.call-start = ((), (), s32[]{:S(2)}) async-start(), calls=%async_computation.14 | async-start | bytes 2654208 | tf_op jit(solution)/shard_map/reduce_scatter | solution.py:260
  281.8 4.5 copy-start.24
  281.8 19.3 %copy-start.26 = (u32[32]{0:T(128)S(1)}, u32[32]{0:T(128)}, u32[]{:S(2)}) copy-start(u32[32]{0:T(128)} %constant.151) | copy-start | bytes 388
  281.8 304.8 %reduce-scatter.22.cloned.1.call-start = ((), (), s32[]{:S(2)}) async-start(), calls=%async_computation.15 | async-start | bytes 2654208 | tf_op jit(solution)/shard_map/reduce_scatter | solution.py:262
  286.2 17.3 %copy-start.6 = (f32[1024,3,64]{0,2,1:T(8,128)S(1)}, f32[1024,3,64]{0,2,1:T(8,128)}, u32[]{:S(2)}) copy-start(f32[1024,3,64]{0,2,1:T(8,128)} %get-tuple-element.152) | copy-start | bytes 2359300
  286.2 98.9 %copy-start = (bf16[1,256,768]{2,1,0:T(8,128)(2,1)S(1)}, bf16[1,256,768]{2,1,0:T(8,128)(2,1)}, u32[]{:S(2)}) copy-start(bf16[1,256,768]{2,1,0:T(8,128)(2,1)} %param.15) | copy-start | bytes 1179652
  286.2 98.9 %copy-start.17 = (f32[768]{0:T(1024)S(1)}, f32[768]{0:T(1024)}, u32[]{:S(2)}) copy-start(f32[768]{0:T(1024)} %copy-done.16) | copy-start | bytes 9220
  286.2 98.9 %copy-start.19 = (f32[256]{0:T(256)S(1)}, f32[256]{0:T(256)}, u32[]{:S(2)}) copy-start(f32[256]{0:T(256)} %copy-done.18) | copy-start | bytes 3076
  286.2 98.9 %copy-start.21 = (f32[256]{0:T(256)S(1)}, f32[256]{0:T(256)}, u32[]{:S(2)}) copy-start(f32[256]{0:T(256)} %copy-done.20) | copy-start | bytes 3076
  286.3 161.5 %copy-start.7 = (bf16[1,256,768]{2,1,0:T(8,128)(2,1)S(1)}, bf16[1,256,768]{2,1,0:T(8,128)(2,1)}, u32[]{:S(2)}) copy-start(bf16[1,256,768]{2,1,0:T(8,128)(2,1)} %param.25) | copy-start | bytes 1179652
  286.3 3.6 collective-permute-start
  290.0 4.5 collective-permute-start.1
  294.5 1.2 collective-permute-start.2
  295.8 3.7 collective-permute-start.3
  299.5 3.8 collective-permute-start.4
Sparse Core Ops, SparseCore 0:
  55.6 36.8 all-gather.5
  94.0 35.8 all-gather.11
  131.8 22.8 all-gather.7
  156.4 24.0 all-gather.9
  251.6 32.5 reduce-scatter.25
  287.2 35.0 reduce-scatter.23
  324.7 60.4 reduce-scatter.15
  387.4 60.2 reduce-scatter.13
  451.7 42.3 reduce-scatter.17
  497.9 42.4 reduce-scatter.19
  544.3 42.3 reduce-scatter.21
